TPU v7x, 32 devices: a whole 2x2x4 slice. The times are simulated.
32 devices in a mesh: dp: 4 (over y, x), ctx: 8 (over z, core).
Axes of the slice: x: 2, y: 2, z: 4, core: 2. Of those that a mesh axis runs over, the one named last changes fastest.
Arguments:
- query_rows: bfloat16 [4, 1024, 1024], P('dp', 'ctx'), may hold values from -0.59765625 to 0.59765625
- key_rows: bfloat16 [4, 1024, 1024], P('dp', 'ctx'), may hold values from -0.59765625 to 0.59765625
- value_rows: bfloat16 [4, 1024, 2048], P('dp', 'ctx'), may hold values from -6 to 6
- log_decay: bfloat16 [4, 1024, 1024], P('dp', 'ctx'), may hold values from -1 to 0, as said below
- out_grad: bfloat16 [4, 1024, 2048], P('dp', 'ctx'), may hold values from -1.796875 to 1.796875
- doc_ids: int32 [4, 1024], P('dp', 'ctx'), may hold values from 0 to 3, as said below
- block_order: int32 [4, 8, 4], P(None, 'ctx'), may hold values from 0 to 3, each once within a row
Outputs:
- attn_out: bfloat16 [4, 1024, 2048], P('dp', 'ctx')
- query_grad: bfloat16 [4, 1024, 1024], P('dp', 'ctx')
- key_grad: bfloat16 [4, 1024, 1024], P('dp', 'ctx')
- value_grad: bfloat16 [4, 1024, 2048], P('dp', 'ctx')
- decay_grad: bfloat16 [4, 1024, 1024], P('dp', 'ctx')
Inputs may be any that keep to these rules, and one draw needn't show every extreme that they name: `log_decay`: nonpositive. `doc_ids`: never falls along a pack; every document number of a pack is used; each document has 1 to 512 positions, one of them exactly 512 and one 8 or fewer. `block_order`: each row of a device's list names each of its 4 blocks once.
All inputs are finite; a program needn't handle non-finite values.
Results may differ from a plain program's by a relative error of at most 0.0015.
Values may be sent and summed in bfloat16 or wider, within the bound.
A program may use at most 192 MiB of HBM per device.

v0:
```python
import jax
import jax.numpy as jnp
from jax import lax
from jax.sharding import PartitionSpec as P

DK = 64
DV = 128
BLK = 32
HIGH = lax.Precision.HIGHEST


def prefix(part, axis, combine, identity, reverse):
    count = lax.axis_size(axis)
    place = lax.axis_index(axis)
    ahead = count - 1 - place if reverse else place
    gathered = jax.tree.map(lambda a: lax.all_gather(a, axis), part)
    state = jax.tree.map(lambda a, e: jnp.zeros_like(a) + jnp.asarray(e, a.dtype), part, identity)

    def one(hop, state):
        source = count - 1 - hop if reverse else hop
        return combine(
            state, jax.tree.map(lambda a: lax.dynamic_index_in_dim(a, source, 0, False), gathered)
        )

    return lax.fori_loop(0, ahead, one, state)


def prepare(query_b, key_b, value_b, decay_b, doc_row):
    row_count = query_b.shape[0]
    head_count = query_b.shape[1] // DK
    query_f = query_b.astype(jnp.float32).reshape(row_count, head_count, DK)
    key_f = key_b.astype(jnp.float32).reshape(row_count, head_count, DK)
    value_f = value_b.astype(jnp.float32).reshape(row_count, head_count, DV)
    cumul = jnp.cumsum(decay_b.astype(jnp.float32).reshape(row_count, head_count, DK), axis=0)
    total_log = cumul[-1]
    growth = jnp.exp(cumul)
    shrink = jnp.exp(-cumul)
    to_end = jnp.exp(total_log[None] - cumul)
    later_pos = lax.broadcasted_iota(jnp.int32, (row_count, row_count), 0)
    earlier_pos = lax.broadcasted_iota(jnp.int32, (row_count, row_count), 1)
    same_doc = ((later_pos >= earlier_pos) & (doc_row[:, None] == doc_row[None, :])).astype(
        jnp.float32
    )
    first_id = doc_row[0]
    last_id = doc_row[-1]
    in_first = (doc_row == first_id).astype(jnp.float32)[:, None, None]
    in_last = (doc_row == last_id).astype(jnp.float32)[:, None, None]
    query_t = query_f * growth
    key_t = key_f * shrink
    scores = jnp.einsum("thi,shi->hts", query_t, key_t, precision=HIGH) * same_doc[None]
    return {
        "query_f": query_f,
        "key_f": key_f,
        "value_f": value_f,
        "growth": growth,
        "shrink": shrink,
        "to_end": to_end,
        "same_doc": same_doc,
        "first_id": first_id,
        "last_id": last_id,
        "in_first": in_first,
        "in_last": in_last,
        "query_t": query_t,
        "key_t": key_t,
        "scores": scores,
        "decay_all": jnp.exp(total_log),
    }


def state_end(parts):
    return jnp.einsum(
        "shi,shj->hij",
        parts["key_f"] * parts["to_end"] * parts["in_last"],
        parts["value_f"],
        precision=HIGH,
    )


def start_grad(parts, grad_f):
    factor = DK ** (-0.5)
    return factor * jnp.einsum(
        "thi,thj->hij", parts["query_t"] * parts["in_first"], grad_f, precision=HIGH
    )


def finish(parts, grad_f, state_in, use_state, carry_in, use_carry):
    factor = DK ** (-0.5)
    head_w = parts["in_first"] * use_state
    tail_w = parts["in_last"] * use_carry
    attn_rows = factor * (
        jnp.einsum("hts,shj->thj", parts["scores"], parts["value_f"], precision=HIGH)
        + jnp.einsum("thi,hij->thj", parts["query_t"], state_in, precision=HIGH) * head_w
    )
    grad_scores = (
        jnp.einsum("thj,shj->hts", grad_f, parts["value_f"], precision=HIGH)
        * parts["same_doc"][None]
    )
    grad_query = (
        factor
        * parts["growth"]
        * (
            jnp.einsum("hts,shi->thi", grad_scores, parts["key_t"], precision=HIGH)
            + jnp.einsum("thj,hij->thi", grad_f, state_in, precision=HIGH) * head_w
        )
    )
    grad_value = (
        factor * jnp.einsum("hts,thj->shj", parts["scores"], grad_f, precision=HIGH)
        + jnp.einsum("shi,hij->shj", parts["key_f"] * parts["to_end"], carry_in, precision=HIGH)
        * tail_w
    )
    grad_key = (
        factor
        * parts["shrink"]
        * jnp.einsum("hts,thi->shi", grad_scores, parts["query_t"], precision=HIGH)
        + parts["to_end"]
        * jnp.einsum("hij,shj->shi", carry_in, parts["value_f"], precision=HIGH)
        * tail_w
    )
    grad_log = parts["query_f"] * grad_query - parts["key_f"] * grad_key
    sum_start = jnp.sum(grad_log * parts["in_first"], axis=0)
    return (attn_rows, grad_query, grad_key, grad_value, grad_log, sum_start)


def decay_grad_of(parts, grad_log, sums_in, use_carry):
    inside = jnp.einsum("ts,thi->shi", parts["same_doc"], grad_log, precision=HIGH)
    return inside + sums_in[None] * parts["in_last"] * use_carry


def select_tree(flag, yes_tree, no_tree):
    return tuple((jnp.where(flag, left, right) for left, right in zip(yes_tree, no_tree)))


def join_forward(before, follow):
    b_dec, b_state, b_first, b_last = before
    f_dec, f_state, f_first, f_last = follow
    joined = ((f_first == f_last) & (b_last == f_first)).astype(jnp.float32)
    merged = (
        f_dec * (joined * b_dec + 1.0 - joined),
        f_state + joined * f_dec[..., None] * b_state,
        b_first,
        f_last,
    )
    return select_tree(b_first < 0, follow, select_tree(f_first < 0, before, merged))


def join_backward(before, follow):
    b_dec, b_state, b_first, b_last = before
    f_dec, f_state, f_first, f_last = follow
    joined = ((f_first == f_last) & (f_last == b_first)).astype(jnp.float32)
    merged = (
        f_dec * (joined * b_dec + 1.0 - joined),
        f_state + joined * f_dec[..., None] * b_state,
        f_first,
        b_last,
    )
    return select_tree(b_first < 0, follow, select_tree(f_first < 0, before, merged))


def join_sums(before, follow):
    b_sum, b_first, b_last = before
    f_sum, f_first, f_last = follow
    joined = ((f_first == f_last) & (f_last == b_first)).astype(jnp.float32)
    merged = (f_sum + joined * b_sum, f_first, b_last)
    return select_tree(b_first < 0, follow, select_tree(f_first < 0, before, merged))


def inverse_of(order_lists):
    block_count = order_lists.shape[-1]
    slot_ids = jnp.arange(block_count, dtype=jnp.int32)
    matches = order_lists[..., :, None] == slot_ids
    return jnp.sum(jnp.where(matches, slot_ids[:, None], 0), axis=-2)


def body(query_rows, key_rows, value_rows, log_decay, out_grad, doc_ids, block_order):
    dp_count = lax.axis_size("dp")
    dp_index = lax.axis_index("dp")
    row_count = query_rows.shape[1]
    block_count = row_count // BLK
    per_peer = block_count // dp_count
    order_lists = block_order[:, 0, :]
    my_order = order_lists[dp_index]
    gathered = (
        lax.all_gather(query_rows, "dp", axis=0, tiled=True),
        lax.all_gather(key_rows, "dp", axis=0, tiled=True),
        lax.all_gather(value_rows, "dp", axis=0, tiled=True),
        lax.all_gather(log_decay, "dp", axis=0, tiled=True),
    )
    inverse = inverse_of(order_lists)
    wanted = dp_index * per_peer + jnp.arange(per_peer, dtype=jnp.int32)
    slot_ids = inverse[:, wanted]
    source_ids = jnp.arange(dp_count, dtype=jnp.int32)[:, None]
    balanced = tuple(
        (
            whole.reshape(dp_count, block_count, BLK, whole.shape[-1])[
                source_ids, slot_ids
            ].reshape(row_count, whole.shape[-1])
            for whole in gathered
        )
    )
    query_bal, key_bal, value_bal, decay_bal = balanced
    doc_row = doc_ids[0]
    parts = prepare(query_bal, key_bal, value_bal, decay_bal, doc_row)
    head_count = parts["query_f"].shape[1]
    grad_f = out_grad[0].astype(jnp.float32).reshape(row_count, head_count, DV)
    first_f = parts["first_id"].astype(jnp.float32)
    last_f = parts["last_id"].astype(jnp.float32)
    neutral = (
        jnp.ones((head_count, DK), jnp.float32),
        jnp.zeros((head_count, DK, DV), jnp.float32),
        jnp.float32(-1.0),
        jnp.float32(-1.0),
    )
    unused_dec, state_in, unused_first, prior_last = prefix(
        (parts["decay_all"], state_end(parts), first_f, last_f), "ctx", join_forward, neutral, False
    )
    use_state = (prior_last == first_f).astype(jnp.float32)
    other_dec, carry_in, next_first, other_last = prefix(
        (parts["decay_all"], start_grad(parts, grad_f), first_f, last_f),
        "ctx",
        join_backward,
        neutral,
        True,
    )
    use_carry = (next_first == last_f).astype(jnp.float32)
    attn_rows, grad_query, grad_key, grad_value, grad_log, sum_start = finish(
        parts, grad_f, state_in, use_state, carry_in, use_carry
    )
    sums_in, later_first, later_last = prefix(
        (sum_start, first_f, last_f),
        "ctx",
        join_sums,
        (jnp.zeros((head_count, DK), jnp.float32), jnp.float32(-1.0), jnp.float32(-1.0)),
        True,
    )
    use_sums = (later_first == last_f).astype(jnp.float32)
    grad_decay = decay_grad_of(parts, grad_log, sums_in, use_sums)
    attn_out = attn_rows.reshape(row_count, head_count * DV).astype(jnp.bfloat16)[None]
    query_back = grad_query.reshape(row_count, head_count * DK).astype(jnp.bfloat16)
    key_back = grad_key.reshape(row_count, head_count * DK).astype(jnp.bfloat16)
    value_back = grad_value.reshape(row_count, head_count * DV).astype(jnp.bfloat16)
    decay_back = grad_decay.reshape(row_count, head_count * DK).astype(jnp.bfloat16)
    gathered_back = (
        lax.all_gather(query_back[None], "dp", axis=0, tiled=True),
        lax.all_gather(key_back[None], "dp", axis=0, tiled=True),
        lax.all_gather(value_back[None], "dp", axis=0, tiled=True),
        lax.all_gather(decay_back[None], "dp", axis=0, tiled=True),
    )
    dest_ids = my_order // per_peer
    dest_slots = dp_index * per_peer + my_order % per_peer
    returned = tuple(
        (
            whole.reshape(dp_count, block_count, BLK, whole.shape[-1])[
                dest_ids, dest_slots
            ].reshape(1, row_count, whole.shape[-1])
            for whole in gathered_back
        )
    )
    query_grad, key_grad, value_grad, decay_grad = returned
    return (attn_out, query_grad, key_grad, value_grad, decay_grad)


def solution(mesh):
    placed = (
        P("dp", "ctx", None),
        P("dp", "ctx", None),
        P("dp", "ctx", None),
        P("dp", "ctx", None),
        P("dp", "ctx", None),
        P("dp", "ctx"),
        P(None, "ctx", None),
    )
    return jax.shard_map(
        body,
        mesh=mesh,
        in_specs=placed,
        out_specs=(
            P("dp", "ctx", None),
            P("dp", "ctx", None),
            P("dp", "ctx", None),
            P("dp", "ctx", None),
            P("dp", "ctx", None),
        ),
        check_vma=False,
    )
```

profile of v0, /device:TPU:0, one launch (start us, length us, event | category | flops | bytes accessed | tf_op | source)
XLA Modules:
  0.0 467.1 jit_solution(8892131721895761153)
XLA Ops:
  15.5 23.7 %all-gather.18.cloned.1.call-done = bf16[4,128,1024]{2,1,0:T(8,128)(2,1)} async-done(((bf16[1,128,1024]{2,1,0:T(8,128)(2,1)}), bf16[4,128,1024]{2,1,0:T(8,128)(2,1)}) %all-gather.18.cloned.1.call-update) | async-done | bytes 1048592 | tf_op jit(solution)/shard_map/all_gather | solution.py:186
  44.1 23.6 %all-gather.16.cloned.1.call-done = bf16[4,128,1024]{2,1,0:T(8,128)(2,1)} async-done(((bf16[1,128,1024]{2,1,0:T(8,128)(2,1)}), bf16[4,128,1024]{2,1,0:T(8,128)(2,1)}) %all-gather.16.cloned.1.call-update) | async-done | bytes 1048592 | tf_op jit(solution)/shard_map/all_gather | solution.py:183
  74.6 21.7 %all-gather.20.cloned.1.call-done = bf16[4,128,1024]{2,1,0:T(8,128)(2,1)} async-done(((bf16[1,128,1024]{2,1,0:T(8,128)(2,1)}), bf16[4,128,1024]{2,1,0:T(8,128)(2,1)}) %all-gather.20.cloned.1.call-update) | async-done | bytes 1048592 | tf_op jit(solution)/shard_map/all_gather | solution.py:184
  101.6 31.6 %all-gather.14.cloned.1.call-done = bf16[4,128,2048]{2,1,0:T(8,128)(2,1)} async-done(((bf16[1,128,2048]{2,1,0:T(8,128)(2,1)}), bf16[4,128,2048]{2,1,0:T(8,128)(2,1)}) %all-gather.14.cloned.1.call-update) | async-done | bytes 2097168 | tf_op jit(solution)/shard_map/all_gather | solution.py:185
  133.3 2.2 gather_fusion
  140.4 17.0 %all-reduce.3 = (f32[8]{0:T(128)S(1)}, f32[8]{0:T(128)S(1)}) all-reduce(f32[8]{0:T(128)S(1)} %dynamic-update-slice.1, f32[8]{0:T(128)S(1)} %dynamic-update-slice.2), channel_id=1, replica_groups=mesh['dp'=4,'ctx'=8] {'ctx'}, use_global_device_ids=true, to_apply=%add.1 | all-reduce | flops 16 | bytes 128
  157.5 14.2 %all_gather.78 = f32[8,16,64]{2,1,0:T(8,128)S(1)} all-gather(f32[1,16,64]{2,1,0:T(8,128)S(1)} %get-tuple-element.421), channel_id=1, replica_groups=mesh['dp'=4,'ctx'=8] {'ctx'}, dimensions={0}, use_global_device_ids=true | all-gather | bytes 36864 | tf_op jit(solution)/shard_map/all_gather | solution.py:16
  173.2 9.4 %all-gather.32.cloned.1.call-done = f32[128,64,128]{2,1,0:T(8,128)} async-done(((f32[16,64,128]{2,1,0:T(8,128)}), f32[128,64,128]{2,1,0:T(8,128)}) %all-gather.32.cloned.1.call-update) | async-done | bytes 4194320 | tf_op jit(solution)/shard_map/all_gather | solution.py:16
  182.6 45.4 %while.51 = (s32[]{:T(128)}, f32[16,64,128]{2,1,0:T(8,128)S(1)}, f32[]{:T(128)}, s32[]{:T(128)}, f32[8,16,64,128]{3,2,1,0:T(8,128)}, /*index=5*/f32[8]{0:T(128)S...) while((s32[]{:T(128)}, f32[16,64,128]{2,1,0:T(8,128)S(1)}, ...), condition=%wide.region_5.6_spmd, body=%wide.region_4.5_spmd.sunk | while | flops 525326 | bytes 1585431 | solution.py:25
  228.0 2.5 all-gather.30.cloned.1.call-done
  233.7 2.2 fusion.12
  239.2 61.9 %all-gather.2 = f32[128,64]{1,0:T(8,128)S(1)} all-gather(f32[16,64]{1,0:T(8,128)S(1)} %get-tuple-element.419), channel_id=4, replica_groups=mesh['dp'=4,'ctx'=8] {'ctx'}, dimensions={0}, use_global_device_ids=true | all-gather | bytes 36864 | tf_op jit(solution)/shard_map/all_gather | solution.py:16
  301.0 34.3 %while.52 = (s32[]{:T(128)}, f32[16,64]{1,0:T(8,128)S(1)}, f32[]{:T(128)}, s32[]{:T(128)}, f32[8,16,64]{2,1,0:T(8,128)S(1)}, /*index=5*/f32[8]{0:T(128)S(1)}, f3...) while((s32[]{:T(128)}, f32[16,64]{1,0:T(8,128)S(1)}, f32[]{:T(128)}, ...), condition=%wide.region_8.9_spmd, body=%wide.region_7.8_spmd.sunk | while | flops 4110 | bytes 12555 | solution.py:25
  341.2 2.9 convolution_multiply_fusion.3
  346.1 2.8 fusion.9
  352.0 2.4 fusion.24
  357.3 5.4 %all-gather.28.cloned.1.call-done = bf16[4,128,1024]{2,1,0:T(8,128)(2,1)} async-done(((bf16[1,128,1024]{2,1,0:T(8,128)(2,1)}), bf16[4,128,1024]{2,1,0:T(8,128)(2,1)}) %all-gather.28.cloned.1.call-update) | async-done | bytes 1048592 | tf_op jit(solution)/shard_map/all_gather | solution.py:246
  362.6 2.5 gather_fusion.7
  365.1 26.0 %all-gather.24.cloned.1.call-done = bf16[4,128,1024]{2,1,0:T(8,128)(2,1)} async-done(((bf16[1,128,1024]{2,1,0:T(8,128)(2,1)}), bf16[4,128,1024]{2,1,0:T(8,128)(2,1)}) %all-gather.24.cloned.1.call-update) | async-done | bytes 1048592 | tf_op jit(solution)/shard_map/all_gather | solution.py:244
  391.1 2.5 gather_fusion.5
  393.6 26.6 %all-gather.22.cloned.1.call-done = bf16[4,128,1024]{2,1,0:T(8,128)(2,1)} async-done(((bf16[1,128,1024]{2,1,0:T(8,128)(2,1)}), bf16[4,128,1024]{2,1,0:T(8,128)(2,1)}) %all-gather.22.cloned.1.call-update) | async-done | bytes 1048592 | tf_op jit(solution)/shard_map/all_gather | solution.py:243
  420.2 2.5 gather_fusion.4
  422.7 34.5 %all-gather.26.cloned.1.call-done = bf16[4,128,2048]{2,1,0:T(8,128)(2,1)} async-done(((bf16[1,128,2048]{2,1,0:T(8,128)(2,1)}), bf16[4,128,2048]{2,1,0:T(8,128)(2,1)}) %all-gather.26.cloned.1.call-update) | async-done | bytes 2097168 | tf_op jit(solution)/shard_map/all_gather | solution.py:245
  457.3 3.0 gather_fusion.6
  (139 shorter events, 78.3 us)
Async XLA Ops:
  7.2 32.0 %all-gather.18.cloned.1.call-start = ((), (), s32[]{:S(2)}) async-start(), calls=%async_computation.2 | async-start | bytes 1310720 | tf_op jit(solution)/shard_map/all_gather | solution.py:186
  7.9 59.8 %all-gather.16.cloned.1.call-start = ((), (), s32[]{:S(2)}) async-start(), calls=%async_computation.1 | async-start | bytes 1310720 | tf_op jit(solution)/shard_map/all_gather | solution.py:183
  8.6 87.6 %all-gather.20.cloned.1.call-start = ((), (), s32[]{:S(2)}) async-start(), calls=%async_computation.3 | async-start | bytes 1310720 | tf_op jit(solution)/shard_map/all_gather | solution.py:184
  9.4 123.9 %all-gather.14.cloned.1.call-start = ((), (), s32[]{:S(2)}) async-start(), calls=%async_computation | async-start | bytes 2621440 | tf_op jit(solution)/shard_map/all_gather | solution.py:185
  10.0 172.6 %all-gather.32.cloned.1.call-start = ((), (), s32[]{:S(2)}) async-start(), calls=%async_computation.9 | async-start | bytes 4718592 | tf_op jit(solution)/shard_map/all_gather | solution.py:16
  43.7 25.8 %copy-start.7 = (f32[128,16,64]{2,1,0:T(8,128)}, f32[128,16,64]{2,1,0:T(8,128)S(1)}, u32[]{:S(2)}) copy-start(f32[128,16,64]{2,1,0:T(8,128)S(1)} %fusion.44) | copy-start | bytes 1572868
  72.4 25.6 %copy-start.5 = (f32[128,16,64]{0,2,1:T(8,128)}, f32[128,16,64]{0,2,1:T(8,128)S(1)}, u32[]{:S(2)}) copy-start(f32[128,16,64]{0,2,1:T(8,128)S(1)} %copy.125) | copy-start | bytes 1572868
  72.5 62.9 %copy-start = (f32[128,16,64]{0,2,1:T(8,128)}, f32[128,16,64]{0,2,1:T(8,128)S(1)}, u32[]{:S(2)}) copy-start(f32[128,16,64]{0,2,1:T(8,128)S(1)} %exponential_multiply_fusion) | copy-start | bytes 1572868
  74.5 63.8 %copy-start.9 = (u32[32]{0:T(128)S(1)}, u32[32]{0:T(128)}, u32[]{:S(2)}) copy-start(u32[32]{0:T(128)} %constant.302) | copy-start | bytes 388
  74.5 82.9 %copy-start.8 = (s32[1,128]{1,0:T(1,128)S(1)}, s32[1,128]{1,0:T(1,128)}, u32[]{:S(2)}) copy-start(s32[1,128]{1,0:T(1,128)} %param.18) | copy-start | bytes 1540
  74.5 156.0 %all-gather.30.cloned.1.call-start = ((), (), s32[]{:S(2)}) async-start(), calls=%async_computation.8 | async-start | bytes 4718592 | tf_op jit(solution)/shard_map/all_gather | solution.py:16
  137.1 225.6 %all-gather.28.cloned.1.call-start = ((), (), s32[]{:S(2)}) async-start(), calls=%async_computation.7 | async-start | bytes 1310720 | tf_op jit(solution)/shard_map/all_gather | solution.py:246
  230.6 3.1 copy-start.3
  230.6 5.2 %copy-start.1 = (f32[128,16,64]{0,2,1:T(8,128)S(1)}, f32[128,16,64]{0,2,1:T(8,128)}, u32[]{:S(2)}) copy-start(f32[128,16,64]{0,2,1:T(8,128)} %copy-done) | copy-start | bytes 1572868
  230.6 5.2 %copy-start.6 = (f32[128,16,64]{0,2,1:T(8,128)S(1)}, f32[128,16,64]{0,2,1:T(8,128)}, u32[]{:S(2)}) copy-start(f32[128,16,64]{0,2,1:T(8,128)} %copy-done.5) | copy-start | bytes 1572868
  337.4 53.7 %all-gather.24.cloned.1.call-start = ((), (), s32[]{:S(2)}) async-start(), calls=%async_computation.5 | async-start | bytes 1310720 | tf_op jit(solution)/shard_map/all_gather | solution.py:244
  339.3 80.9 %all-gather.22.cloned.1.call-start = ((), (), s32[]{:S(2)}) async-start(), calls=%async_computation.4 | async-start | bytes 1310720 | tf_op jit(solution)/shard_map/all_gather | solution.py:243
  341.2 116.1 %all-gather.26.cloned.1.call-start = ((), (), s32[]{:S(2)}) async-start(), calls=%async_computation.6 | async-start | bytes 2621440 | tf_op jit(solution)/shard_map/all_gather | solution.py:245
  344.1 1.0 copy-start.4
  346.1 8.3 %copy-start.2 = (f32[128,16,64]{0,2,1:T(8,128)S(1)}, f32[128,16,64]{0,2,1:T(8,128)}, u32[]{:S(2)}) copy-start(f32[128,16,64]{0,2,1:T(8,128)} %copy-done) | copy-start | bytes 1572868
Sparse Core Ops, SparseCore 0:
  9.8 29.3 all-gather.17
  41.0 26.6 all-gather.15
  69.6 26.6 all-gather.19
  97.9 35.2 all-gather.13
  134.7 47.8 all-gather.31
  184.6 45.8 all-gather.29
  337.6 25.0 all-gather.27
  364.5 26.6 all-gather.23
  393.6 26.6 all-gather.21
  421.9 35.2 all-gather.25
where the time goes:
time: 469 us; the launch traced here: 467 us
  waiting for transfers between devices  208 us (44%)
  blocking collectives  93 us (20%)
  local copies, waits for them, and re-layouts  57.1 us (12%)
  loops' own time  52.2 us (11%)
  matrix products  23.1 us (5%)
  other arithmetic  18 us (4%)
  between operations  15.7 us (3%)
    all_gather x2, blocking collectives, prefix(): gathered = jax.tree.map(lambda a: lax.all_gather(a, axis), part)  76 us
    another operation x3, loops' own time, prefix(): return lax.fori_loop(0, ahead, one, state)  52.2 us
    all_gather x1, waiting for transfers between devices, body(): lax.all_gather(value_back[None], 'dp', axis=0, tiled=True)  34.5 us
    all_gather x1, waiting for transfers between devices, body(): lax.all_gather(value_rows, 'dp', axis=0, tiled=True)  31.6 us
    all_gather x1, waiting for transfers between devices, body(): lax.all_gather(query_back[None], 'dp', axis=0, tiled=True)  26.6 us
    all_gather x1, waiting for transfers between devices, body(): lax.all_gather(key_back[None], 'dp', axis=0, tiled=True)  26 us
    all_gather x1, waiting for transfers between devices, body(): lax.all_gather(log_decay, 'dp', axis=0, tiled=True)  23.7 us
    all_gather x1, waiting for transfers between devices, body(): lax.all_gather(query_rows, 'dp', axis=0, tiled=True)  23.6 us
  transfers between devices with their start and end apart: 10, of which 10 were waited for; matrix products, arithmetic and copies ran while one was open for 16% of the time, Pallas kernels for 0%

commit v1 on v0

--- a/solution.py
+++ b/solution.py
@@ -239,8 +239,31 @@
     key_back = grad_key.reshape(row_count, head_count * DK).astype(jnp.bfloat16)
     value_back = grad_value.reshape(row_count, head_count * DV).astype(jnp.bfloat16)
     decay_back = grad_decay.reshape(row_count, head_count * DK).astype(jnp.bfloat16)
+
+    def quarters_view(axis_tag, slab_in):
+        z_new = lax.axis_size(axis_tag)
+        shaped = lax.axis_index(axis_tag)
+        lower, block_next, outer = (z_new, shaped, slab_in.shape[0])
+        chunks = list(map(lambda src_i: (src_i, (src_i + 1) % lower), range(lower)))
+        runs = list(map(lambda src_i: (src_i, (src_i - 1) % lower), range(lower)))
+        left_arr = jnp.zeros((*slab_in.shape[:0], lower * outer, *slab_in.shape[1:]), slab_in.dtype)
+        left_arr = lax.dynamic_update_slice_in_dim(left_arr, slab_in, block_next * outer, axis=0)
+        kept_arr = wide_out = slab_in
+        current_value = lower // 2
+        for j in range(1, current_value + 1):
+            kept_arr = lax.ppermute(kept_arr, axis_name=axis_tag, perm=chunks)
+            left_arr = lax.dynamic_update_slice_in_dim(
+                left_arr, kept_arr, (block_next - j) % lower * outer, axis=0
+            )
+            if j < lower - current_value:
+                wide_out = lax.ppermute(wide_out, axis_name=axis_tag, perm=runs)
+                left_arr = lax.dynamic_update_slice_in_dim(
+                    left_arr, wide_out, (block_next + j) % lower * outer, axis=0
+                )
+        return left_arr
+
     gathered_back = (
-        lax.all_gather(query_back[None], "dp", axis=0, tiled=True),
+        quarters_view("dp", query_back[None]),
         lax.all_gather(key_back[None], "dp", axis=0, tiled=True),
         lax.all_gather(value_back[None], "dp", axis=0, tiled=True),
         lax.all_gather(decay_back[None], "dp", axis=0, tiled=True),

time: 469 us -> 444 us (0.947)
  waiting for transfers between devices: 208 us -> 159 us
  other arithmetic: 18 us -> 39.9 us
  starting transfers between devices: 0.4 us -> 5.52 us
    all_gather x1 -> x0, waiting for transfers between devices: 26.6 us -> none  [body(): lax.all_gather(query_back[None], 'dp', axis=0, tiled=True)]
    another operation x1, other arithmetic: 1.36 us -> 23.3 us  [prepare(): jnp.cumsum(decay_b.astype(jnp.float32).reshape(row_count, head_count, DK)...]
    all_gather x1, waiting for transfers between devices: 23.6 us -> 2.68 us  [body(): lax.all_gather(query_rows, 'dp', axis=0, tiled=True)]
    ppermute x0 -> x3, waiting for transfers between devices: none -> 13.7 us  [the longest x2 12.4 us: quarters_view(): kept_arr = lax.ppermute(kept_arr, axis_name=axis_tag, perm=chunks)]
    all_gather x1, waiting for transfers between devices: 26 us -> 16.4 us  [body(): lax.all_gather(key_back[None], 'dp', axis=0, tiled=True)]
    all_gather x1, waiting for transfers between devices: 5.38 us -> 0.01 us  [body(): lax.all_gather(decay_back[None], 'dp', axis=0, tiled=True)]
    ppermute x0 -> x3, starting transfers between devices: none -> 5.16 us  [the longest x2 3.58 us: quarters_view(): kept_arr = lax.ppermute(kept_arr, axis_name=axis_tag, perm=chunks)]
  transfers between devices with their start and end apart: 10 -> 12, of which waited for: 10 -> 11; matrix products, arithmetic and copies ran while one was open for 16% -> 21% of each run, Pallas kernels for 0% -> 0%
where the time goes in v1:
time: 444 us; the launch traced here: 442 us
  waiting for transfers between devices  159 us (36%)
  blocking collectives  93 us (21%)
  local copies, waits for them, and re-layouts  53.6 us (12%)
  loops' own time  52.2 us (12%)
  other arithmetic  39.9 us (9%)
  matrix products  23.1 us (5%)
  between operations  15.5 us (3%)
  starting transfers between devices  5.52 us (1%)
    all_gather x2, blocking collectives, prefix(): gathered = jax.tree.map(lambda a: lax.all_gather(a, axis), part)  76 us
    another operation x3, loops' own time, prefix(): return lax.fori_loop(0, ahead, one, state)  52.2 us
    all_gather x1, waiting for transfers between devices, body(): lax.all_gather(value_back[None], 'dp', axis=0, tiled=True)  34.7 us
    all_gather x1, waiting for transfers between devices, body(): lax.all_gather(value_rows, 'dp', axis=0, tiled=True)  32.3 us
    all_gather x1, waiting for transfers between devices, body(): lax.all_gather(log_decay, 'dp', axis=0, tiled=True)  23.7 us
    another operation x1, other arithmetic, prepare(): jnp.cumsum(decay_b.astype(jnp.float32).reshape(row_count, head_count, DK)...  23.3 us
    all_gather x1, waiting for transfers between devices, body(): lax.all_gather(key_rows, 'dp', axis=0, tiled=True)  20.8 us
    unnamed x1, blocking collectives  17 us
  transfers between devices with their start and end apart: 12, of which 11 were waited for; matrix products, arithmetic and copies ran while one was open for 21% of the time, Pallas kernels for 0%

profile of v1, /device:TPU:0, one launch (start us, length us, event | category | flops | bytes accessed | tf_op | source)
XLA Modules:
  0.0 441.7 jit_solution(8101787578206000379)
XLA Ops:
  15.5 23.7 %all-gather.17.cloned.1.call-done = bf16[4,128,1024]{2,1,0:T(8,128)(2,1)} async-done(((bf16[1,128,1024]{2,1,0:T(8,128)(2,1)}), bf16[4,128,1024]{2,1,0:T(8,128)(2,1)}) %all-gather.17.cloned.1.call-update) | async-done | bytes 1048592 | tf_op jit(solution)/shard_map/all_gather | solution.py:186
  41.3 23.3 %fusion.41 = f32[128,16,64]{2,1,0:T(8,128)S(1)} fusion(f32[128,16,64]{2,1,0:T(8,128)S(1)} %reshape.327), kind=kOutput, calls=%fused_computation.88 | output fusion | flops 16646144 | bytes 1048576 | tf_op jit(solution)/shard_map/jit(cumsum)/reduce_window_sum | solution.py:34
  65.0 2.7 all-gather.15.cloned.1.call-done
  75.4 20.8 %all-gather.19.cloned.1.call-done = bf16[4,128,1024]{2,1,0:T(8,128)(2,1)} async-done(((bf16[1,128,1024]{2,1,0:T(8,128)(2,1)}), bf16[4,128,1024]{2,1,0:T(8,128)(2,1)}) %all-gather.19.cloned.1.call-update) | async-done | bytes 1048592 | tf_op jit(solution)/shard_map/all_gather | solution.py:184
  100.9 32.3 %all-gather.13.cloned.1.call-done = bf16[4,128,2048]{2,1,0:T(8,128)(2,1)} async-done(((bf16[1,128,2048]{2,1,0:T(8,128)(2,1)}), bf16[4,128,2048]{2,1,0:T(8,128)(2,1)}) %all-gather.13.cloned.1.call-update) | async-done | bytes 2097168 | tf_op jit(solution)/shard_map/all_gather | solution.py:185
  133.3 2.2 gather_fusion
  140.4 17.0 %all-reduce.3 = (f32[8]{0:T(128)S(1)}, f32[8]{0:T(128)S(1)}) all-reduce(f32[8]{0:T(128)S(1)} %dynamic-update-slice.1, f32[8]{0:T(128)S(1)} %dynamic-update-slice.2), channel_id=1, replica_groups=mesh['dp'=4,'ctx'=8] {'ctx'}, use_global_device_ids=true, to_apply=%add.1 | all-reduce | flops 16 | bytes 128
  157.5 14.2 %all_gather.75 = f32[8,16,64]{2,1,0:T(8,128)S(1)} all-gather(f32[1,16,64]{2,1,0:T(8,128)S(1)} %get-tuple-element.421), channel_id=1, replica_groups=mesh['dp'=4,'ctx'=8] {'ctx'}, dimensions={0}, use_global_device_ids=true | all-gather | bytes 36864 | tf_op jit(solution)/shard_map/all_gather | solution.py:16
  173.2 9.4 %all-gather.29.cloned.1.call-done = f32[128,64,128]{2,1,0:T(8,128)} async-done(((f32[16,64,128]{2,1,0:T(8,128)}), f32[128,64,128]{2,1,0:T(8,128)}) %all-gather.29.cloned.1.call-update) | async-done | bytes 4194320 | tf_op jit(solution)/shard_map/all_gather | solution.py:16
  182.6 45.4 %while.51 = (s32[]{:T(128)}, f32[16,64,128]{2,1,0:T(8,128)S(1)}, f32[]{:T(128)}, s32[]{:T(128)}, f32[8,16,64,128]{3,2,1,0:T(8,128)}, /*index=5*/f32[8]{0:T(128)S...) while((s32[]{:T(128)}, f32[16,64,128]{2,1,0:T(8,128)S(1)}, ...), condition=%wide.region_5.6_spmd, body=%wide.region_4.5_spmd.sunk | while | flops 525326 | bytes 1585431 | solution.py:25
  228.0 2.5 all-gather.27.cloned.1.call-done
  239.2 61.8 %all-gather.2 = f32[128,64]{1,0:T(8,128)S(1)} all-gather(f32[16,64]{1,0:T(8,128)S(1)} %get-tuple-element.419), channel_id=4, replica_groups=mesh['dp'=4,'ctx'=8] {'ctx'}, dimensions={0}, use_global_device_ids=true | all-gather | bytes 36864 | tf_op jit(solution)/shard_map/all_gather | solution.py:16
  301.0 34.3 %while.52 = (s32[]{:T(128)}, f32[16,64]{1,0:T(8,128)S(1)}, f32[]{:T(128)}, s32[]{:T(128)}, f32[8,16,64]{2,1,0:T(8,128)S(1)}, /*index=5*/f32[8]{0:T(128)S(1)}, f3...) while((s32[]{:T(128)}, f32[16,64]{1,0:T(8,128)S(1)}, f32[]{:T(128)}, ...), condition=%wide.region_8.9_spmd, body=%wide.region_7.8_spmd.sunk | while | flops 4110 | bytes 12555 | solution.py:25
  339.4 2.9 convolution_multiply_fusion.3
  344.3 2.8 fusion.9
  350.3 2.4 fusion.24
  357.6 9.1 %collective-permute-done = bf16[1,128,1024]{2,1,0:T(8,128)(2,1)S(1)} collective-permute-done((bf16[1,128,1024]{2,1,0:T(8,128)(2,1)S(1)}, bf16[1,128,1024]{2,1,0:T(8,128)(2,1)S(1)}, u32[]{:S(2)}, u32[]{:S(2)}) %collective-permute-start) | collective-permute-done | bytes 262176 | tf_op jit(solution)/shard_map/ppermute | solution.py:254
  366.7 2.2 collective-permute-start.2
  371.4 3.3 collective-permute-done.2
  376.0 2.5 gather_fusion.7
  378.5 16.4 %all-gather.21.cloned.1.call-done = bf16[4,128,1024]{2,1,0:T(8,128)(2,1)} async-done(((bf16[1,128,1024]{2,1,0:T(8,128)(2,1)}), bf16[4,128,1024]{2,1,0:T(8,128)(2,1)}) %all-gather.21.cloned.1.call-update) | async-done | bytes 1048592 | tf_op jit(solution)/shard_map/all_gather | solution.py:267
  395.0 2.5 gather_fusion.5
  397.5 34.7 %all-gather.23.cloned.1.call-done = bf16[4,128,2048]{2,1,0:T(8,128)(2,1)} async-done(((bf16[1,128,2048]{2,1,0:T(8,128)(2,1)}), bf16[4,128,2048]{2,1,0:T(8,128)(2,1)}) %all-gather.23.cloned.1.call-update) | async-done | bytes 2097168 | tf_op jit(solution)/shard_map/all_gather | solution.py:268
  432.2 3.0 gather_fusion.6
  (147 shorter events, 82.3 us)
Async XLA Ops:
  7.2 32.0 %all-gather.17.cloned.1.call-start = ((), (), s32[]{:S(2)}) async-start(), calls=%async_computation.2 | async-start | bytes 1310720 | tf_op jit(solution)/shard_map/all_gather | solution.py:186
  7.9 59.8 %all-gather.15.cloned.1.call-start = ((), (), s32[]{:S(2)}) async-start(), calls=%async_computation.1 | async-start | bytes 1310720 | tf_op jit(solution)/shard_map/all_gather | solution.py:183
  8.6 87.6 %all-gather.19.cloned.1.call-start = ((), (), s32[]{:S(2)}) async-start(), calls=%async_computation.3 | async-start | bytes 1310720 | tf_op jit(solution)/shard_map/all_gather | solution.py:184
  9.4 123.9 %all-gather.13.cloned.1.call-start = ((), (), s32[]{:S(2)}) async-start(), calls=%async_computation | async-start | bytes 2621440 | tf_op jit(solution)/shard_map/all_gather | solution.py:185
  10.0 172.6 %all-gather.29.cloned.1.call-start = ((), (), s32[]{:S(2)}) async-start(), calls=%async_computation.8 | async-start | bytes 4718592 | tf_op jit(solution)/shard_map/all_gather | solution.py:16
  72.4 63.0 %copy-start.5 = (f32[128,16,64]{0,2,1:T(8,128)}, f32[128,16,64]{0,2,1:T(8,128)S(1)}, u32[]{:S(2)}) copy-start(f32[128,16,64]{0,2,1:T(8,128)S(1)} %copy.133) | copy-start | bytes 1572868
  72.5 0.9 copy-start
  75.3 63.0 %copy-start.9 = (u32[32]{0:T(128)S(1)}, u32[32]{0:T(128)}, u32[]{:S(2)}) copy-start(u32[32]{0:T(128)} %constant.328) | copy-start | bytes 388
  75.3 82.1 %copy-start.8 = (s32[1,128]{1,0:T(1,128)S(1)}, s32[1,128]{1,0:T(1,128)}, u32[]{:S(2)}) copy-start(s32[1,128]{1,0:T(1,128)} %param.18) | copy-start | bytes 1540
  75.3 155.2 %all-gather.27.cloned.1.call-start = ((), (), s32[]{:S(2)}) async-start(), calls=%async_computation.7 | async-start | bytes 4718592 | tf_op jit(solution)/shard_map/all_gather | solution.py:16
  137.1 239.0 %all-gather.25.cloned.1.call-start = ((), (), s32[]{:S(2)}) async-start(), calls=%async_computation.6 | async-start | bytes 1310720 | tf_op jit(solution)/shard_map/all_gather | solution.py:269
  230.6 3.1 copy-start.3
  230.6 5.2 %copy-start.1 = (f32[128,16,64]{0,2,1:T(8,128)S(1)}, f32[128,16,64]{0,2,1:T(8,128)}, u32[]{:S(2)}) copy-start(f32[128,16,64]{0,2,1:T(8,128)} %copy-done) | copy-start | bytes 1572868
  230.6 5.2 %copy-start.6 = (f32[128,16,64]{0,2,1:T(8,128)S(1)}, f32[128,16,64]{0,2,1:T(8,128)}, u32[]{:S(2)}) copy-start(f32[128,16,64]{0,2,1:T(8,128)} %copy-done.5) | copy-start | bytes 1572868
  337.5 57.5 %all-gather.21.cloned.1.call-start = ((), (), s32[]{:S(2)}) async-start(), calls=%async_computation.4 | async-start | bytes 1310720 | tf_op jit(solution)/shard_map/all_gather | solution.py:267
  339.3 92.8 %all-gather.23.cloned.1.call-start = ((), (), s32[]{:S(2)}) async-start(), calls=%async_computation.5 | async-start | bytes 2621440 | tf_op jit(solution)/shard_map/all_gather | solution.py:268
  342.3 1.0 copy-start.4
  344.3 8.3 %copy-start.7 = (bf16[128,16,64]{0,2,1:T(8,128)(2,1)S(1)}, bf16[128,16,64]{0,2,1:T(8,128)(2,1)}, u32[]{:S(2)}) copy-start(bf16[128,16,64]{0,2,1:T(8,128)(2,1)} %get-tuple-element.423) | copy-start | bytes 786436
  344.3 11.5 %copy-start.2 = (f32[128,16,64]{0,2,1:T(8,128)S(1)}, f32[128,16,64]{0,2,1:T(8,128)}, u32[]{:S(2)}) copy-start(f32[128,16,64]{0,2,1:T(8,128)} %copy-done) | copy-start | bytes 1572868
  352.8 13.9 %collective-permute-start = (bf16[1,128,1024]{2,1,0:T(8,128)(2,1)S(1)}, bf16[1,128,1024]{2,1,0:T(8,128)(2,1)S(1)}, u32[]{:S(2)}, u32[]{:S(2)}) collective-permute-start(bf16[1,128,1024]{2,1,0:T(8,128)(2,1)S(1)} %copy.144), channel_id=1, source_target_pairs={{0,8},{8,16},{16,24},{24,0},{1,9},{9,17},{17,25},{25,1},{2,10},{10... | collective-permute-start | bytes 786440 | tf_op jit(solution)/shard_map/ppermute | solution.py:254
  354.2 17.1 %collective-permute-start.1 = (bf16[1,128,1024]{2,1,0:T(8,128)(2,1)S(1)}, bf16[1,128,1024]{2,1,0:T(8,128)(2,1)S(1)}, u32[]{:S(2)}, u32[]{:S(2)}) collective-permute-start(bf16[1,128,1024]{2,1,0:T(8,128)(2,1)S(1)} %copy.144), channel_id=1, source_target_pairs={{0,24},{8,0},{16,8},{24,16},{1,25},{9,1},{17,9},{25,17},{2,26},{10... | collective-permute-start | bytes 786440 | tf_op jit(solution)/shard_map/ppermute | solution.py:259
  366.7 8.0 %collective-permute-start.2 = (bf16[1,128,1024]{2,1,0:T(8,128)(2,1)S(1)}, bf16[1,128,1024]{2,1,0:T(8,128)(2,1)S(1)}, u32[]{:S(2)}, u32[]{:S(2)}) collective-permute-start(bf16[1,128,1024]{2,1,0:T(8,128)(2,1)S(1)} %collective-permute-done), channel_id=1, source_target_pairs={{0,8},{8,16},{16,24},{24,0},{1,9},{9,17},{17,25},{25,1},{2,10},{10... | collective-permute-start | bytes 786440 | tf_op jit(solution)/shard_map/ppermute | solution.py:254
Sparse Core Ops, SparseCore 0:
  9.8 29.3 all-gather.16
  41.0 26.6 all-gather.14
  69.6 26.6 all-gather.18
  97.9 35.2 all-gather.12
  134.7 47.8 all-gather.28
  184.6 45.8 all-gather.26
  337.6 31.5 all-gather.24
  371.0 23.9 all-gather.20
  396.8 35.2 all-gather.22
